TPU v7x, 32 devices: a whole 2x2x4 slice. The times are simulated.
32 devices in a mesh: row: 8 (over z, x), col: 4 (over y, core).
Axes of the slice: x: 2, y: 2, z: 4, core: 2. Of those that a mesh axis runs over, the one named last changes fastest.
Arguments:
- tokens: bfloat16 [512, 8192], P('col', 'row'), may hold values from -6 to 6
- gate_weight: bfloat16 [8192, 14336], P('row', 'col'), may hold values from -0.09375 to 0.09375
- up_weight: bfloat16 [8192, 14336], P('row', 'col'), may hold values from -0.09375 to 0.09375
- down_weight: bfloat16 [14336, 8192], P('col', 'row'), may hold values from -0.09375 to 0.09375
- gate_mask: int32 [128, 224], P('row', 'col'), may hold values from 0 to 1, as said below
- up_mask: int32 [128, 224], P('row', 'col'), may hold values from 0 to 1, as said below
- down_mask: int32 [224, 128], P('col', 'row'), may hold values from 0 to 1, as said below
- head_weight: bfloat16 [8192, 128], P('row'), may hold values from -0.15625 to 0.15625
- labels: int32 [512], P('col'), may hold values from 0 to 127
Outputs:
- token_loss: float32 [512], P('col')
- tokens_grad: bfloat16 [512, 8192], P('col', 'row')
- gate_grad: bfloat16 [8192, 14336], P('row', 'col')
- up_grad: bfloat16 [8192, 14336], P('row', 'col')
- down_grad: bfloat16 [14336, 8192], P('col', 'row')
Inputs may be any that keep to these rules, and one draw needn't show every extreme that they name: `gate_mask`: 1 keeps a block of 64 x 64 weights, 0 prunes it. `up_mask`: 1 keeps a block of 64 x 64 weights, 0 prunes it. `down_mask`: 1 keeps a block of 64 x 64 weights, 0 prunes it.
All inputs are finite; a program needn't handle non-finite values.
Results may differ from a plain program's by a relative error of at most 0.011.
Values may be sent and summed in bfloat16 or wider, within the bound.
A program may use at most 192 MiB of HBM per device.

v0:
```python
import jax
import jax.numpy as jnp
from jax import lax
from jax.sharding import PartitionSpec as P

loss_scale = 8.0


def masked(weight, block_mask):
    height, breadth = weight.shape
    blocks = weight.reshape(
        block_mask.shape[0],
        height // block_mask.shape[0],
        block_mask.shape[1],
        breadth // block_mask.shape[1],
    )
    pruned = blocks * block_mask[:, None, :, None].astype(weight.dtype)
    return pruned.reshape(height, breadth)


def classify(logits, labels):
    exponent = jnp.exp(logits)
    partition = jnp.sum(exponent, axis=1, keepdims=True)
    classes = lax.broadcasted_iota(jnp.int32, logits.shape, 1)
    onehot = (labels[:, None] == classes).astype(jnp.float32)
    token_cost = jnp.log(partition[:, 0]) - jnp.sum(logits * onehot, axis=1)
    return (token_cost, loss_scale * (exponent / partition - onehot))


def token_product(panel_rows, weight, weight_axis):
    panel_axis = 0
    return lax.dot_general(
        panel_rows,
        weight,
        (((panel_axis,), (weight_axis,)), ((), ())),
        preferred_element_type=jnp.float32,
    )


def shards(
    tokens, gate_weight, up_weight, down_weight, gate_mask, up_mask, down_mask, head_weight, labels
):
    gate_kept = masked(gate_weight, gate_mask)
    up_kept = masked(up_weight, up_mask)
    down_kept = masked(down_weight, down_mask)
    every_token = lax.all_gather(tokens, "col", axis=0, tiled=True)
    gate_part = lax.dot_general(
        gate_kept, every_token, (((0,), (1,)), ((), ())), preferred_element_type=jnp.float32
    )
    up_part = lax.dot_general(
        up_kept, every_token, (((0,), (1,)), ((), ())), preferred_element_type=jnp.float32
    )
    stacked = lax.psum_scatter(
        jnp.concatenate([gate_part, up_part], axis=1), "row", scatter_dimension=0, tiled=True
    )
    midpoint = stacked.shape[1] // 2
    gate_sum = stacked[:, :midpoint]
    up_sum = stacked[:, midpoint:]
    sigmoid_gate = jax.nn.sigmoid(gate_sum)
    activated = gate_sum * sigmoid_gate
    hidden = (activated * up_sum).astype(jnp.bfloat16)
    hidden_all = lax.all_gather(hidden, "row", axis=0, tiled=True)
    branch = lax.psum_scatter(
        token_product(hidden_all, down_kept, 0), "col", scatter_dimension=0, tiled=True
    )
    mixed_rows = (tokens.astype(jnp.float32) + branch).astype(jnp.bfloat16)
    partial_value = jnp.dot(mixed_rows, head_weight, preferred_element_type=jnp.float32)
    logits = lax.psum(partial_value, "row")
    token_loss, grad_full = classify(logits, labels)
    dlogits = grad_full.astype(jnp.bfloat16)
    dmixed = lax.dot_general(
        dlogits, head_weight, (((1,), (1,)), ((), ())), preferred_element_type=jnp.float32
    ).astype(jnp.bfloat16)
    dmixed_all = lax.all_gather(dmixed, "col", axis=0, tiled=True)
    dhidden = lax.psum_scatter(
        lax.dot_general(
            down_kept, dmixed_all, (((1,), (1,)), ((), ())), preferred_element_type=jnp.float32
        ),
        "row",
        scatter_dimension=0,
        tiled=True,
    )
    gate_delta = (dhidden * up_sum * sigmoid_gate * (1.0 + gate_sum * (1.0 - sigmoid_gate))).astype(
        jnp.bfloat16
    )
    up_delta = (dhidden * activated).astype(jnp.bfloat16)
    gate_all, up_all = (
        lax.all_gather(gate_delta, "row", axis=0, tiled=True),
        lax.all_gather(up_delta, "row", axis=0, tiled=True),
    )
    token_axis = 1
    down_grad = masked(
        lax.dot_general(
            hidden_all,
            dmixed_all,
            (((token_axis,), (0,)), ((), ())),
            preferred_element_type=jnp.float32,
        ),
        down_mask,
    ).astype(jnp.bfloat16)
    gate_grad = masked(
        lax.dot_general(
            every_token,
            gate_all,
            (((0,), (token_axis,)), ((), ())),
            preferred_element_type=jnp.float32,
        ),
        gate_mask,
    ).astype(jnp.bfloat16)
    up_grad = masked(
        lax.dot_general(
            every_token,
            up_all,
            (((0,), (token_axis,)), ((), ())),
            preferred_element_type=jnp.float32,
        ),
        up_mask,
    ).astype(jnp.bfloat16)
    gate_term = token_product(gate_all, gate_kept, 1)
    up_term = token_product(up_all, up_kept, 1)
    input_sum = lax.psum_scatter(gate_term + up_term, "col", scatter_dimension=0, tiled=True)
    tokens_grad = (dmixed.astype(jnp.float32) + input_sum).astype(jnp.bfloat16)
    return (token_loss, tokens_grad, gate_grad, up_grad, down_grad)


def solution(mesh):
    placed = (
        P("col", "row"),
        P("row", "col"),
        P("row", "col"),
        P("col", "row"),
        P("row", "col"),
        P("row", "col"),
        P("col", "row"),
        P("row", None),
        P("col"),
    )
    return jax.shard_map(
        shards,
        mesh=mesh,
        in_specs=placed,
        out_specs=(P("col"), P("col", "row"), P("row", "col"), P("row", "col"), P("col", "row")),
        check_vma=False,
    )
```

profile of v0, /device:TPU:0, one launch (start us, length us, event | category | flops | bytes accessed | tf_op | source)
XLA Modules:
  0.0 1011.9 jit_solution(17688586089172399964)
XLA Ops:
  7.2 0.7 all-gather.6.cloned.1.call-update
  8.0 0.8 fusion.9
  8.7 7.2 mul.99
  15.9 18.9 %mul.100 = bf16[1024,3584]{1,0:T(8,128)(2,1)} reshape(bf16[16,64,56,64]{3,2,1,0:T(8,128)(2,1)} %mul.99) | data formatting | bytes 14680064 | tf_op jit(solution)/shard_map/mul | solution.py:17
  34.9 7.2 mul.96
  42.0 18.7 %mul.97 = bf16[1024,3584]{1,0:T(8,128)(2,1)} reshape(bf16[16,64,56,64]{3,2,1,0:T(8,128)(2,1)} %mul.96) | data formatting | bytes 14680064 | tf_op jit(solution)/shard_map/mul | solution.py:17
  60.8 10.2 %mul.101 = bf16[1024,3584]{1,0:T(8,128)(2,1)} multiply(bf16[1024,3584]{1,0:T(8,128)(2,1)} %param.11, bf16[1024,3584]{1,0:T(8,128)(2,1)} %mul.100) | non-fusion elementwise | flops 3670016 | bytes 22020096 | tf_op jit(solution)/shard_map/mul | solution.py:17
  71.0 10.2 %mul.98 = bf16[1024,3584]{1,0:T(8,128)(2,1)} multiply(bf16[1024,3584]{1,0:T(8,128)(2,1)} %param.10, bf16[1024,3584]{1,0:T(8,128)(2,1)} %mul.97) | non-fusion elementwise | flops 3670016 | bytes 22020096 | tf_op jit(solution)/shard_map/mul | solution.py:17
  81.2 6.6 fusion.15
  87.8 4.0 fusion.14
  91.8 5.5 pad_maximum_fusion
  97.3 15.7 %copy.43 = f32[3584,1024]{1,0:T(8,128)} copy(f32[3584,1024]{0,1:T(8,128)} %pad_maximum_fusion) | data formatting | bytes 29360128
  113.1 239.5 %reduce-scatter.13.cloned.1.call-done = f32[448,1024]{1,0:T(8,128)} async-done(((f32[3584,1024]{1,0:T(8,128)}), f32[448,1024]{1,0:T(8,128)}) %reduce-scatter.13.cloned.1.call-update) | async-done | bytes 1835024 | tf_op jit(solution)/shard_map/reduce_scatter | solution.py:53
  352.6 2.5 multiply_convert_fusion.3
  355.2 0.1 copy.33
  355.3 7.2 mul.104
  362.5 20.1 %mul.105 = bf16[3584,1024]{1,0:T(8,128)(2,1)} reshape(bf16[56,64,16,64]{3,2,1,0:T(8,128)(2,1)} %mul.104) | data formatting | bytes 14680064 | tf_op jit(solution)/shard_map/mul | solution.py:17
  382.6 12.5 %mul.106 = bf16[3584,1024]{1,0:T(8,128)(2,1)} multiply(bf16[3584,1024]{1,0:T(8,128)(2,1)} %param.12, bf16[3584,1024]{1,0:T(8,128)(2,1)} %mul.105) | non-fusion elementwise | flops 3670016 | bytes 22020096 | tf_op jit(solution)/shard_map/mul | solution.py:17
  395.1 25.5 %all-gather.8.cloned.1.call-done = bf16[3584,512]{1,0:T(8,128)(2,1)} async-done(((bf16[448,512]{1,0:T(8,128)(2,1)}), bf16[3584,512]{1,0:T(8,128)(2,1)}) %all-gather.8.cloned.1.call-update) | async-done | bytes 3670032 | tf_op jit(solution)/shard_map/all_gather | solution.py:62
  420.6 9.5 fusion.11
  430.2 30.0 %reduce-scatter.9.cloned.1.call-done = f32[128,1024]{1,0:T(8,128)} async-done(((f32[512,1024]{1,0:T(8,128)}), f32[128,1024]{1,0:T(8,128)}) %reduce-scatter.9.cloned.1.call-update) | async-done | bytes 524304 | tf_op jit(solution)/shard_map/reduce_scatter | solution.py:63
  460.2 1.9 fusion.3
  462.1 71.2 %all-reduce.2.cloned.1.call-done = f32[128,128]{1,0:T(8,128)} async-done(((f32[128,128]{1,0:T(8,128)}), f32[128,128]{1,0:T(8,128)}) %all-reduce.2.cloned.1.call-update) | async-done | bytes 65552 | tf_op jit(solution)/shard_map/psum | solution.py:68
  533.3 1.0 exponential_reduce_fusion
  534.3 1.8 convolution_convert_fusion
  536.2 0.2 reduce-scatter.15.cloned.1.call-start
  536.4 16.6 %all-gather.10.cloned.1.call-done = bf16[512,1024]{1,0:T(8,128)(2,1)} async-done(((bf16[128,1024]{1,0:T(8,128)(2,1)}), bf16[512,1024]{1,0:T(8,128)(2,1)}) %all-gather.10.cloned.1.call-update) | async-done | bytes 1048592 | tf_op jit(solution)/shard_map/all_gather | solution.py:74
  553.0 10.3 %fusion.12 = f32[3584,512]{1,0:T(8,128)} fusion(bf16[3584,1024]{1,0:T(8,128)(2,1)} %mul.106, bf16[512,1024]{1,0:T(8,128)(2,1)} %all-gather.10.cloned.1.call-done), kind=kOutput, calls=%fused_computation.29 | convolution fusion | flops 3758096384 | bytes 15728640
  563.3 133.0 %reduce-scatter.15.cloned.1.call-done = f32[448,512]{1,0:T(8,128)} async-done(((f32[3584,512]{1,0:T(8,128)}), f32[448,512]{1,0:T(8,128)}) %reduce-scatter.15.cloned.1.call-update) | async-done | bytes 917520 | tf_op jit(solution)/shard_map/reduce_scatter | solution.py:75
  696.3 2.6 multiply_convert_fusion.1
  699.0 0.7 all-gather.14.cloned.1.call-update
  699.7 64.6 %all-gather.12.cloned.1.call-done = bf16[3584,512]{1,0:T(8,128)(2,1)} async-done(((bf16[448,512]{1,0:T(8,128)(2,1)}), bf16[3584,512]{1,0:T(8,128)(2,1)}) %all-gather.12.cloned.1.call-update) | async-done | bytes 3670032 | tf_op jit(solution)/shard_map/all_gather | solution.py:88
  764.4 9.5 fusion.13
  773.9 57.6 %all-gather.14.cloned.1.call-done = bf16[3584,512]{1,0:T(8,128)(2,1)} async-done(((bf16[448,512]{1,0:T(8,128)(2,1)}), bf16[3584,512]{1,0:T(8,128)(2,1)}) %all-gather.14.cloned.1.call-update) | async-done | bytes 3670032 | tf_op jit(solution)/shard_map/all_gather | solution.py:89
  831.5 10.1 convolution_add_fusion
  841.9 12.7 %mul.115 = f32[16,64,56,64]{1,0,3,2:T(8,128)} broadcast(f32[16,56]{0,1:T(8,128)S(1)} %copy.37), dimensions={0,2} | broadcast | bytes 14683648 | tf_op jit(solution)/shard_map/mul | solution.py:17
  854.6 25.2 %mul.116 = f32[1024,3584]{0,1:T(8,128)} reshape(f32[16,64,56,64]{1,0,3,2:T(8,128)} %mul.115) | data formatting | bytes 29360128 | tf_op jit(solution)/shard_map/mul | solution.py:17
  879.8 11.6 %mul.118 = f32[16,64,56,64]{1,0,3,2:T(8,128)} broadcast(f32[16,56]{0,1:T(8,128)S(1)} %copy.38), dimensions={0,2} | broadcast | bytes 14683648 | tf_op jit(solution)/shard_map/mul | solution.py:17
  891.4 24.9 %mul.119 = f32[1024,3584]{0,1:T(8,128)} reshape(f32[16,64,56,64]{1,0,3,2:T(8,128)} %mul.118) | data formatting | bytes 29360128 | tf_op jit(solution)/shard_map/mul | solution.py:17
  916.3 11.6 %mul.121 = f32[56,64,16,64]{3,2,1,0:T(8,128)} broadcast(f32[56,16]{1,0:T(8,128)S(1)} %copy.39), dimensions={0,2} | broadcast | bytes 14683648 | tf_op jit(solution)/shard_map/mul | solution.py:17
  928.0 25.0 %mul.122 = f32[3584,1024]{1,0:T(8,128)} reshape(f32[56,64,16,64]{3,2,1,0:T(8,128)} %mul.121) | data formatting | bytes 29360128 | tf_op jit(solution)/shard_map/mul | solution.py:17
  953.0 0.5 log_subtract_fusion
  953.5 10.3 %multiply_convert_fusion = bf16[3584,1024]{1,0:T(8,128)(2,1)} fusion(f32[3584,1024]{1,0:T(8,128)} %mul.122, bf16[3584,512]{1,0:T(8,128)(2,1)} %all-gather.8.cloned.1.call-done, bf16[512,1024]{1,0:T(8,128)(2,1)S(1)} %copy-done.8), kind=kOutput, calls=%fused_computation.5 | convolution fusion | flops 3765436416 | bytes 26738688 | tf_op jit(solution)/shard_map/dot_general | solution.py:93
  963.8 9.1 fusion.1
  972.9 9.9 copy.40
  982.8 10.2 %fusion = bf16[1024,3584]{0,1:T(8,128)(2,1)} fusion(f32[1024,3584]{0,1:T(8,128)} %mul.119, bf16[3584,512]{1,0:T(8,128)(2,1)} %all-gather.14.cloned.1.call-done, bf16[512,1024]{1,0:T(8,128)(2,1)S(1)} %copy-done.5), kind=kOutput, calls=%fused_computation.2 | convolution fusion | flops 3765436416 | bytes 26738688 | tf_op jit(solution)/shard_map/dot_general | solution.py:111
  993.0 10.0 copy.41
  1003.0 1.8 add_convert_fusion
  (48 shorter events, 0.8 us)
Async XLA Ops:
  7.2 453.0 %copy-start = (bf16[1024,128]{1,0:T(8,128)(2,1)S(1)}, bf16[1024,128]{1,0:T(8,128)(2,1)}, u32[]{:S(2)}) copy-start(bf16[1024,128]{1,0:T(8,128)(2,1)} %param.16) | copy-start | bytes 786436
  7.2 74.0 %all-gather.6.cloned.1.call-start = ((), (), s32[]{:S(2)}) async-start(), calls=%async_computation.4 | async-start | bytes 1310720 | tf_op jit(solution)/shard_map/all_gather | solution.py:46
  7.9 344.7 %reduce-scatter.13.cloned.1.call-start = ((), (), s32[]{:S(2)}) async-start(), calls=%async_computation.12 | async-start | bytes 16515072 | tf_op jit(solution)/shard_map/reduce_scatter | solution.py:53
  15.9 18.9 %copy-start.9 = (s32[16,56]{1,0:T(8,128)S(1)}, s32[16,56]{1,0:T(8,128)}, u32[]{:S(2)}) copy-start(s32[16,56]{1,0:T(8,128)} %param.13) | copy-start | bytes 10756
  81.2 6.7 copy-start.4
  81.2 6.7 copy-start.5
  113.0 242.2 %copy-start.10 = (s32[56,16]{0,1:T(8,128)S(1)}, s32[56,16]{0,1:T(8,128)}, u32[]{:S(2)}) copy-start(s32[56,16]{0,1:T(8,128)} %param.15) | copy-start | bytes 10756
  113.0 307.6 %all-gather.8.cloned.1.call-start = ((), (), s32[]{:S(2)}) async-start(), calls=%async_computation.5 | async-start | bytes 4128768 | tf_op jit(solution)/shard_map/all_gather | solution.py:62
  355.1 105.0 %reduce-scatter.9.cloned.1.call-start = ((), (), s32[]{:S(2)}) async-start(), calls=%async_computation.6 | async-start | bytes 2621440 | tf_op jit(solution)/shard_map/reduce_scatter | solution.py:63
  395.1 65.1 %copy-start.7 = (bf16[128,1024]{1,0:T(8,128)(2,1)S(1)}, bf16[128,1024]{1,0:T(8,128)(2,1)}, u32[]{:S(2)}) copy-start(bf16[128,1024]{1,0:T(8,128)(2,1)} %param.9) | copy-start | bytes 786436
  395.1 138.2 %copy-start.11 = (s32[128]{0:T(128)S(1)}, s32[128]{0:T(128)}, u32[]{:S(2)}) copy-start(s32[128]{0:T(128)} %param.17) | copy-start | bytes 1540
  430.1 103.2 %all-reduce.2.cloned.1.call-start = ((), (), s32[]{:S(2)}) async-start(), calls=%async_computation.7 | async-start | bytes 131072 | tf_op jit(solution)/shard_map/psum | solution.py:68
  462.1 90.9 %all-gather.10.cloned.1.call-start = ((), (), s32[]{:S(2)}) async-start(), calls=%async_computation.8 | async-start | bytes 1310720 | tf_op jit(solution)/shard_map/all_gather | solution.py:74
  536.2 160.1 %reduce-scatter.15.cloned.1.call-start = ((), (), s32[]{:S(2)}) async-start(), calls=%async_computation.13 | async-start | bytes 8257536 | tf_op jit(solution)/shard_map/reduce_scatter | solution.py:75
  563.2 133.1 %copy-start.3 = (f32[448,1024]{1,0:T(8,128)S(1)}, f32[448,1024]{1,0:T(8,128)}, u32[]{:S(2)}) copy-start(f32[448,1024]{1,0:T(8,128)} %reduce-scatter.13.cloned.1.call-done) | copy-start | bytes 5505028
  563.3 201.1 %all-gather.12.cloned.1.call-start = ((), (), s32[]{:S(2)}) async-start(), calls=%async_computation.9 | async-start | bytes 4128768 | tf_op jit(solution)/shard_map/all_gather | solution.py:88
  699.0 132.6 %all-gather.14.cloned.1.call-start = ((), (), s32[]{:S(2)}) async-start(), calls=%async_computation.10 | async-start | bytes 4128768 | tf_op jit(solution)/shard_map/all_gather | solution.py:89
  699.7 303.3 %reduce-scatter.11.cloned.1.call-start = ((), (), s32[]{:S(2)}) async-start(), calls=%async_computation.11 | async-start | bytes 2621440 | tf_op jit(solution)/shard_map/reduce_scatter | solution.py:121
  928.0 25.5 %copy-start.8 = (bf16[512,1024]{1,0:T(8,128)(2,1)S(1)}, bf16[512,1024]{1,0:T(8,128)(2,1)}, u32[]{:S(2)}) copy-start(bf16[512,1024]{1,0:T(8,128)(2,1)} %all-gather.10.cloned.1.call-done) | copy-start | bytes 3145732
  953.5 10.3 %copy-start.2 = (bf16[3584,512]{1,0:T(8,128)(2,1)S(1)}, bf16[3584,512]{1,0:T(8,128)(2,1)}, u32[]{:S(2)}) copy-start(bf16[3584,512]{1,0:T(8,128)(2,1)} %all-gather.12.cloned.1.call-done) | copy-start | bytes 11010052
  982.8 22.0 %copy-start.1 = (bf16[1024,128]{1,0:T(8,128)(2,1)S(1)}, bf16[1024,128]{1,0:T(8,128)(2,1)}, u32[]{:S(2)}) copy-start(bf16[1024,128]{1,0:T(8,128)(2,1)} %param.16) | copy-start | bytes 786436
  993.0 10.0 copy-start.6
Sparse Core Ops, SparseCore 0:
  9.5 19.4 all-gather.5
  113.2 239.4 reduce-scatter.12
  355.3 65.2 all-gather.7
  430.2 29.8 reduce-scatter.8
  464.0 69.2 all-reduce.1
  536.3 16.6 all-gather.9
  563.4 132.8 reduce-scatter.14
  699.1 65.2 all-gather.11
  766.6 64.9 all-gather.13
  841.8 29.8 reduce-scatter.10
where the time goes:
time: 1020 us; the launch traced here: 1010 us
  waiting for transfers between devices  640 us (63%)
  local copies, waits for them, and re-layouts  226 us (22%)
  matrix products  83.3 us (8%)
  other arithmetic  47.7 us (5%)
  between operations  14.5 us (1%)
    reduce_scatter x1, waiting for transfers between devices, shards(): lax.psum_scatter(jnp.concatenate([gate_part, up_part], axis=1), 'row', sc...  240 us
    mul x12, local copies, waits for them, and re-layouts, masked(): pruned = blocks * block_mask[:, None, :, None].astype(weight.dtype)  190 us
    reduce_scatter x1, waiting for transfers between devices, shards(): lax.psum_scatter(lax.dot_general(down_kept, dmixed_all, (((1,), (1,)), ((...  133 us
    psum x1, waiting for transfers between devices, shards(): logits = lax.psum(partial_value, 'row')  71.2 us
    all_gather x1, waiting for transfers between devices, shards(): lax.all_gather(gate_delta, 'row', axis=0, tiled=True)  64.6 us
    all_gather x1, waiting for transfers between devices, shards(): lax.all_gather(up_delta, 'row', axis=0, tiled=True)  57.6 us
    unnamed x27, local copies, waits for them, and re-layouts  35.6 us
    mul x3, other arithmetic, masked(): pruned = blocks * block_mask[:, None, :, None].astype(weight.dtype)  32.9 us
  transfers between devices with their start and end apart: 10, of which 8 were waited for; matrix products, arithmetic and copies ran while one was open for 28% of the time, Pallas kernels for 0%

commit v1 on v0

--- a/solution.py
+++ b/solution.py
@@ -65,7 +65,7 @@
     )
     mixed_rows = (tokens.astype(jnp.float32) + branch).astype(jnp.bfloat16)
     partial_value = jnp.dot(mixed_rows, head_weight, preferred_element_type=jnp.float32)
-    logits = lax.psum(partial_value, "row")
+    logits = jax.lax.all_gather(partial_value, "row").sum(axis=0)
     token_loss, grad_full = classify(logits, labels)
     dlogits = grad_full.astype(jnp.bfloat16)
     dmixed = lax.dot_general(

time: 1020 us -> 976 us (0.957)
  waiting for transfers between devices: 640 us -> 568 us
  blocking collectives: 0 us -> 31.5 us
    psum x1 -> x0, waiting for transfers between devices: 71.2 us -> none  [shards(): logits = lax.psum(partial_value, 'row')]
    all_gather x0 -> x1, blocking collectives: none -> 31.5 us  [shards(): logits = jax.lax.all_gather(partial_value, 'row').sum(axis=0)]
  transfers between devices with their start and end apart: 10 -> 9, of which waited for: 8 -> 7; matrix products, arithmetic and copies ran while one was open for 28% -> 29% of each run, Pallas kernels for 0% -> 0%
where the time goes in v1:
time: 976 us; the launch traced here: 970 us
  waiting for transfers between devices  568 us (58%)
  local copies, waits for them, and re-layouts  226 us (23%)
  matrix products  81.9 us (8%)
  other arithmetic  46.8 us (5%)
  blocking collectives  31.5 us (3%)
  between operations  14.2 us (1%)
    reduce_scatter x1, waiting for transfers between devices, shards(): lax.psum_scatter(jnp.concatenate([gate_part, up_part], axis=1), 'row', sc...  240 us
    mul x12, local copies, waits for them, and re-layouts, masked(): pruned = blocks * block_mask[:, None, :, None].astype(weight.dtype)  190 us
    reduce_scatter x1, waiting for transfers between devices, shards(): lax.psum_scatter(lax.dot_general(down_kept, dmixed_all, (((1,), (1,)), ((...  133 us
    all_gather x1, waiting for transfers between devices, shards(): lax.all_gather(gate_delta, 'row', axis=0, tiled=True)  64.6 us
    all_gather x1, waiting for transfers between devices, shards(): lax.all_gather(up_delta, 'row', axis=0, tiled=True)  57.6 us
    unnamed x27, local copies, waits for them, and re-layouts  35.7 us
    mul x3, other arithmetic, masked(): pruned = blocks * block_mask[:, None, :, None].astype(weight.dtype)  32.9 us
    all_gather x1, blocking collectives, shards(): logits = jax.lax.all_gather(partial_value, 'row').sum(axis=0)  31.5 us
  transfers between devices with their start and end apart: 9, of which 7 were waited for; matrix products, arithmetic and copies ran while one was open for 29% of the time, Pallas kernels for 0%

profile of v1, /device:TPU:0, one launch (start us, length us, event | category | flops | bytes accessed | tf_op | source)
XLA Modules:
  0.0 969.6 jit_solution(13632425199118753057)
XLA Ops:
  7.2 0.7 all-gather.7.cloned.1.call-update
  8.0 0.8 fusion.9
  8.7 7.2 mul.99
  15.9 18.9 %mul.100 = bf16[1024,3584]{1,0:T(8,128)(2,1)} reshape(bf16[16,64,56,64]{3,2,1,0:T(8,128)(2,1)} %mul.99) | data formatting | bytes 14680064 | tf_op jit(solution)/shard_map/mul | solution.py:17
  34.9 7.2 mul.96
  42.1 18.7 %mul.97 = bf16[1024,3584]{1,0:T(8,128)(2,1)} reshape(bf16[16,64,56,64]{3,2,1,0:T(8,128)(2,1)} %mul.96) | data formatting | bytes 14680064 | tf_op jit(solution)/shard_map/mul | solution.py:17
  60.8 10.2 %mul.101 = bf16[1024,3584]{1,0:T(8,128)(2,1)} multiply(bf16[1024,3584]{1,0:T(8,128)(2,1)} %param.11, bf16[1024,3584]{1,0:T(8,128)(2,1)} %mul.100) | non-fusion elementwise | flops 3670016 | bytes 22020096 | tf_op jit(solution)/shard_map/mul | solution.py:17
  71.0 10.2 %mul.98 = bf16[1024,3584]{1,0:T(8,128)(2,1)} multiply(bf16[1024,3584]{1,0:T(8,128)(2,1)} %param.10, bf16[1024,3584]{1,0:T(8,128)(2,1)} %mul.97) | non-fusion elementwise | flops 3670016 | bytes 22020096 | tf_op jit(solution)/shard_map/mul | solution.py:17
  81.2 6.6 fusion.15
  87.9 4.0 fusion.14
  91.8 5.4 pad_maximum_fusion
  97.3 15.7 %copy.53 = f32[3584,1024]{1,0:T(8,128)} copy(f32[3584,1024]{0,1:T(8,128)} %pad_maximum_fusion) | data formatting | bytes 29360128
  113.0 239.5 %reduce-scatter.13.cloned.1.call-done = f32[448,1024]{1,0:T(8,128)} async-done(((f32[3584,1024]{1,0:T(8,128)}), f32[448,1024]{1,0:T(8,128)}) %reduce-scatter.13.cloned.1.call-update) | async-done | bytes 1835024 | tf_op jit(solution)/shard_map/reduce_scatter | solution.py:53
  352.6 2.5 multiply_convert_fusion.3
  355.1 0.1 copy.43
  355.2 7.2 mul.104
  362.4 20.1 %mul.105 = bf16[3584,1024]{1,0:T(8,128)(2,1)} reshape(bf16[56,64,16,64]{3,2,1,0:T(8,128)(2,1)} %mul.104) | data formatting | bytes 14680064 | tf_op jit(solution)/shard_map/mul | solution.py:17
  382.5 12.5 %mul.106 = bf16[3584,1024]{1,0:T(8,128)(2,1)} multiply(bf16[3584,1024]{1,0:T(8,128)(2,1)} %param.12, bf16[3584,1024]{1,0:T(8,128)(2,1)} %mul.105) | non-fusion elementwise | flops 3670016 | bytes 22020096 | tf_op jit(solution)/shard_map/mul | solution.py:17
  395.0 25.5 %all-gather.9.cloned.1.call-done = bf16[3584,512]{1,0:T(8,128)(2,1)} async-done(((bf16[448,512]{1,0:T(8,128)(2,1)}), bf16[3584,512]{1,0:T(8,128)(2,1)}) %all-gather.9.cloned.1.call-update) | async-done | bytes 3670032 | tf_op jit(solution)/shard_map/all_gather | solution.py:62
  420.5 9.5 fusion.11
  430.1 30.0 %reduce-scatter.9.cloned.1.call-done = f32[128,1024]{1,0:T(8,128)} async-done(((f32[512,1024]{1,0:T(8,128)}), f32[128,1024]{1,0:T(8,128)}) %reduce-scatter.9.cloned.1.call-update) | async-done | bytes 524304 | tf_op jit(solution)/shard_map/reduce_scatter | solution.py:63
  460.1 1.3 fusion.3
  461.4 31.5 %all-gather = f32[1024,128]{1,0:T(8,128)S(1)} all-gather(f32[128,128]{1,0:T(8,128)S(1)} %fusion.3), channel_id=2, replica_groups=mesh['row'=8,'col'=4] {'row'}, dimensions={0}, use_global_device_ids=true | all-gather | bytes 589824 | tf_op jit(solution)/shard_map/all_gather | solution.py:68
  492.9 0.2 exponential_reduce_fusion
  493.1 1.0 convolution_convert_fusion
  494.1 0.2 reduce-scatter.15.cloned.1.call-start
  494.3 16.7 %all-gather.11.cloned.1.call-done = bf16[512,1024]{1,0:T(8,128)(2,1)} async-done(((bf16[128,1024]{1,0:T(8,128)(2,1)}), bf16[512,1024]{1,0:T(8,128)(2,1)}) %all-gather.11.cloned.1.call-update) | async-done | bytes 1048592 | tf_op jit(solution)/shard_map/all_gather | solution.py:74
  511.0 10.3 %fusion.12 = f32[3584,512]{1,0:T(8,128)} fusion(bf16[3584,1024]{1,0:T(8,128)(2,1)} %mul.106, bf16[512,1024]{1,0:T(8,128)(2,1)} %all-gather.11.cloned.1.call-done), kind=kOutput, calls=%fused_computation.29 | convolution fusion | flops 3758096384 | bytes 15728640
  521.3 133.0 %reduce-scatter.15.cloned.1.call-done = f32[448,512]{1,0:T(8,128)} async-done(((f32[3584,512]{1,0:T(8,128)}), f32[448,512]{1,0:T(8,128)}) %reduce-scatter.15.cloned.1.call-update) | async-done | bytes 917520 | tf_op jit(solution)/shard_map/reduce_scatter | solution.py:75
  654.3 2.6 multiply_convert_fusion.1
  657.0 0.7 all-gather.15.cloned.1.call-update
  657.8 64.6 %all-gather.13.cloned.1.call-done = bf16[3584,512]{1,0:T(8,128)(2,1)} async-done(((bf16[448,512]{1,0:T(8,128)(2,1)}), bf16[3584,512]{1,0:T(8,128)(2,1)}) %all-gather.13.cloned.1.call-update) | async-done | bytes 3670032 | tf_op jit(solution)/shard_map/all_gather | solution.py:88
  722.4 9.5 fusion.13
  731.9 57.6 %all-gather.15.cloned.1.call-done = bf16[3584,512]{1,0:T(8,128)(2,1)} async-done(((bf16[448,512]{1,0:T(8,128)(2,1)}), bf16[3584,512]{1,0:T(8,128)(2,1)}) %all-gather.15.cloned.1.call-update) | async-done | bytes 3670032 | tf_op jit(solution)/shard_map/all_gather | solution.py:89
  789.5 10.1 %convolution_add_fusion = f32[512,1024]{1,0:T(8,128)} fusion(f32[512,1024]{1,0:T(8,128)} %fusion.13, bf16[3584,512]{1,0:T(8,128)(2,1)} %all-gather.15.cloned.1.call-done, bf16[1024,3584]{1,0:T(8,128)(2,1)} %mul.101), kind=kOutput, calls=%fused_computation.6 | convolution fusion | flops 3758620672 | bytes 15204352 | tf_op jit(solution)/shard_map/dot_general | solution.py:32
  799.9 12.7 %mul.115 = f32[16,64,56,64]{1,0,3,2:T(8,128)} broadcast(f32[16,56]{0,1:T(8,128)S(1)} %copy.47), dimensions={0,2} | broadcast | bytes 14683648 | tf_op jit(solution)/shard_map/mul | solution.py:17
  812.6 25.2 %mul.116 = f32[1024,3584]{0,1:T(8,128)} reshape(f32[16,64,56,64]{1,0,3,2:T(8,128)} %mul.115) | data formatting | bytes 29360128 | tf_op jit(solution)/shard_map/mul | solution.py:17
  837.8 11.6 %mul.118 = f32[16,64,56,64]{1,0,3,2:T(8,128)} broadcast(f32[16,56]{0,1:T(8,128)S(1)} %copy.48), dimensions={0,2} | broadcast | bytes 14683648 | tf_op jit(solution)/shard_map/mul | solution.py:17
  849.4 24.9 %mul.119 = f32[1024,3584]{0,1:T(8,128)} reshape(f32[16,64,56,64]{1,0,3,2:T(8,128)} %mul.118) | data formatting | bytes 29360128 | tf_op jit(solution)/shard_map/mul | solution.py:17
  874.4 11.6 %mul.121 = f32[56,64,16,64]{3,2,1,0:T(8,128)} broadcast(f32[56,16]{1,0:T(8,128)S(1)} %copy.49), dimensions={0,2} | broadcast | bytes 14683648 | tf_op jit(solution)/shard_map/mul | solution.py:17
  886.0 25.0 %mul.122 = f32[3584,1024]{1,0:T(8,128)} reshape(f32[56,64,16,64]{3,2,1,0:T(8,128)} %mul.121) | data formatting | bytes 29360128 | tf_op jit(solution)/shard_map/mul | solution.py:17
  911.0 0.5 log_subtract_fusion
  911.5 10.3 %multiply_convert_fusion = bf16[3584,1024]{1,0:T(8,128)(2,1)} fusion(f32[3584,1024]{1,0:T(8,128)} %mul.122, bf16[3584,512]{1,0:T(8,128)(2,1)} %all-gather.9.cloned.1.call-done, bf16[512,1024]{1,0:T(8,128)(2,1)S(1)} %copy-done.8), kind=kOutput, calls=%fused_computation.5 | convolution fusion | flops 3765436416 | bytes 26738688 | tf_op jit(solution)/shard_map/dot_general | solution.py:93
  921.8 9.1 fusion.1
  930.9 9.9 %copy.50 = bf16[1024,3584]{1,0:T(8,128)(2,1)} copy(bf16[1024,3584]{0,1:T(8,128)(2,1)} %fusion.1) | data formatting | bytes 14680064
  940.8 10.3 %fusion = bf16[1024,3584]{0,1:T(8,128)(2,1)} fusion(f32[1024,3584]{0,1:T(8,128)} %mul.119, bf16[3584,512]{1,0:T(8,128)(2,1)} %all-gather.15.cloned.1.call-done, bf16[512,1024]{1,0:T(8,128)(2,1)S(1)} %copy-done.5), kind=kOutput, calls=%fused_computation.2 | convolution fusion | flops 3765436416 | bytes 26738688 | tf_op jit(solution)/shard_map/dot_general | solution.py:111
  951.1 10.0 %copy.51 = bf16[1024,3584]{1,0:T(8,128)(2,1)} copy(bf16[1024,3584]{0,1:T(8,128)(2,1)} %fusion) | data formatting | bytes 14680064
  961.0 1.8 add_convert_fusion
  (47 shorter events, 0.8 us)
Async XLA Ops:
  7.2 452.9 %copy-start = (bf16[1024,128]{1,0:T(8,128)(2,1)S(1)}, bf16[1024,128]{1,0:T(8,128)(2,1)}, u32[]{:S(2)}) copy-start(bf16[1024,128]{1,0:T(8,128)(2,1)} %param.16) | copy-start | bytes 786436
  7.2 74.0 %all-gather.7.cloned.1.call-start = ((), (), s32[]{:S(2)}) async-start(), calls=%async_computation.4 | async-start | bytes 1310720 | tf_op jit(solution)/shard_map/all_gather | solution.py:46
  7.9 344.6 %reduce-scatter.13.cloned.1.call-start = ((), (), s32[]{:S(2)}) async-start(), calls=%async_computation.11 | async-start | bytes 16515072 | tf_op jit(solution)/shard_map/reduce_scatter | solution.py:53
  15.9 18.9 %copy-start.9 = (s32[16,56]{1,0:T(8,128)S(1)}, s32[16,56]{1,0:T(8,128)}, u32[]{:S(2)}) copy-start(s32[16,56]{1,0:T(8,128)} %param.13) | copy-start | bytes 10756
  81.2 6.7 copy-start.4
  81.2 6.7 copy-start.5
  113.0 242.1 %copy-start.10 = (s32[56,16]{0,1:T(8,128)S(1)}, s32[56,16]{0,1:T(8,128)}, u32[]{:S(2)}) copy-start(s32[56,16]{0,1:T(8,128)} %param.15) | copy-start | bytes 10756
  113.0 307.5 %all-gather.9.cloned.1.call-start = ((), (), s32[]{:S(2)}) async-start(), calls=%async_computation.5 | async-start | bytes 4128768 | tf_op jit(solution)/shard_map/all_gather | solution.py:62
  355.1 105.0 %reduce-scatter.9.cloned.1.call-start = ((), (), s32[]{:S(2)}) async-start(), calls=%async_computation.6 | async-start | bytes 2621440 | tf_op jit(solution)/shard_map/reduce_scatter | solution.py:63
  395.0 65.1 %copy-start.7 = (bf16[128,1024]{1,0:T(8,128)(2,1)S(1)}, bf16[128,1024]{1,0:T(8,128)(2,1)}, u32[]{:S(2)}) copy-start(bf16[128,1024]{1,0:T(8,128)(2,1)} %param.9) | copy-start | bytes 786436
  395.0 97.9 %copy-start.11 = (s32[128]{0:T(128)S(1)}, s32[128]{0:T(128)}, u32[]{:S(2)}) copy-start(s32[128]{0:T(128)} %param.17) | copy-start | bytes 1540
  430.0 81.0 %all-gather.11.cloned.1.call-start = ((), (), s32[]{:S(2)}) async-start(), calls=%async_computation.7 | async-start | bytes 1310720 | tf_op jit(solution)/shard_map/all_gather | solution.py:74
  494.1 160.2 %reduce-scatter.15.cloned.1.call-start = ((), (), s32[]{:S(2)}) async-start(), calls=%async_computation.12 | async-start | bytes 8257536 | tf_op jit(solution)/shard_map/reduce_scatter | solution.py:75
  521.3 133.1 %copy-start.3 = (f32[448,1024]{1,0:T(8,128)S(1)}, f32[448,1024]{1,0:T(8,128)}, u32[]{:S(2)}) copy-start(f32[448,1024]{1,0:T(8,128)} %reduce-scatter.13.cloned.1.call-done) | copy-start | bytes 5505028
  521.3 201.1 %all-gather.13.cloned.1.call-start = ((), (), s32[]{:S(2)}) async-start(), calls=%async_computation.8 | async-start | bytes 4128768 | tf_op jit(solution)/shard_map/all_gather | solution.py:88
  657.0 132.6 %all-gather.15.cloned.1.call-start = ((), (), s32[]{:S(2)}) async-start(), calls=%async_computation.9 | async-start | bytes 4128768 | tf_op jit(solution)/shard_map/all_gather | solution.py:89
  657.7 303.3 %reduce-scatter.11.cloned.1.call-start = ((), (), s32[]{:S(2)}) async-start(), calls=%async_computation.10 | async-start | bytes 2621440 | tf_op jit(solution)/shard_map/reduce_scatter | solution.py:121
  886.0 25.5 %copy-start.8 = (bf16[512,1024]{1,0:T(8,128)(2,1)S(1)}, bf16[512,1024]{1,0:T(8,128)(2,1)}, u32[]{:S(2)}) copy-start(bf16[512,1024]{1,0:T(8,128)(2,1)} %all-gather.11.cloned.1.call-done) | copy-start | bytes 3145732
  911.5 10.3 %copy-start.2 = (bf16[3584,512]{1,0:T(8,128)(2,1)S(1)}, bf16[3584,512]{1,0:T(8,128)(2,1)}, u32[]{:S(2)}) copy-start(bf16[3584,512]{1,0:T(8,128)(2,1)} %all-gather.13.cloned.1.call-done) | copy-start | bytes 11010052
  940.8 22.0 %copy-start.1 = (bf16[1024,128]{1,0:T(8,128)(2,1)S(1)}, bf16[1024,128]{1,0:T(8,128)(2,1)}, u32[]{:S(2)}) copy-start(bf16[1024,128]{1,0:T(8,128)(2,1)} %param.16) | copy-start | bytes 786436
  951.1 10.0 %copy-start.6 = (bf16[128,1024]{1,0:T(8,128)(2,1)S(1)}, bf16[128,1024]{1,0:T(8,128)(2,1)}, u32[]{:S(2)}) copy-start(bf16[128,1024]{1,0:T(8,128)(2,1)} %convolution_convert_fusion) | copy-start | bytes 786436
Sparse Core Ops, SparseCore 0:
  9.5 19.4 all-gather.6
  113.1 239.3 reduce-scatter.12
  355.2 65.2 all-gather.8
  430.2 29.8 reduce-scatter.8
  494.2 16.7 all-gather.10
  521.4 132.8 reduce-scatter.14
  657.1 65.2 all-gather.12
  724.6 64.9 all-gather.14
  799.8 29.8 reduce-scatter.10
